TPU v7x, 32 devices: a whole 2x2x4 slice. The times are simulated.
32 devices in a mesh: fsdp: 4 (over z), tp: 4 (over y, core), sect: 2 (over x).
Axes of the slice: x: 2, y: 2, z: 4, core: 2. Of those that a mesh axis runs over, the one named last changes fastest.
Arguments:
- hidden: bfloat16 [4096, 8192], P('fsdp', 'sect'), may hold values from -6 to 6
- kv_weight: bfloat16 [8192, 2048], P(('sect', 'fsdp'), 'tp'), may hold values from -0.0625 to 0.0625
- readout: float32 [2048], P(('tp', 'sect')), may hold values from -0.125 to 0.125
- lengths: int32 [4, 4], P('fsdp'), may hold values from 1 to 512, as said below
- prompt_mask: int32 [4096], P('fsdp'), may hold values from 0 to 1, as said below
- group_ids: int32 [16], P('fsdp'), may hold values from 0 to 1
Outputs:
- keys_values: bfloat16 [4096, 2048], P('fsdp', ('tp', 'sect'))
- advantages: float32 [16], P('fsdp')
Inputs may be any that keep to these rules, and one draw needn't show every extreme that they name: `lengths`: each row sums to 1024; some entry of each row equals 512. `prompt_mask`: within each sequence the zeros come before the ones; at each index of fsdp exactly one sequence has no ones.
All inputs are finite; a program needn't handle non-finite values.
Results may differ from a plain program's by a relative error of at most 0.00045.
Values may be sent and summed in bfloat16 or wider, within the bound.
A program may use at most 64 MiB of HBM per device.

v0:
```python
import jax
import jax.numpy as jnp
from jax import lax
from jax.sharding import PartitionSpec as P


def swapped(value, axis, bit):
    mask = 2**bit
    pairs = [(source, source ^ mask) for source in range(lax.axis_size(axis))]
    return lax.ppermute(value, axis, pairs)


def local(hidden, kv_weight, readout, lengths, prompt_mask, group_ids):
    block_width = kv_weight.shape[1]
    col_width = block_width // lax.axis_size("sect")
    sect_index = lax.axis_index("sect")
    tok_rows = hidden.shape[0]

    def add_rows(piece):
        return jnp.dot(hidden, piece, preferred_element_type=jnp.float32)

    partner_cols = lax.dynamic_slice_in_dim(kv_weight, (1 - sect_index) * col_width, col_width, 1)
    partner_part = add_rows(lax.all_gather(partner_cols, "fsdp", axis=0, tiled=True))
    received = swapped(partner_part, "sect", 0)
    own_cols = lax.dynamic_slice_in_dim(kv_weight, sect_index * col_width, col_width, 1)
    own_part = add_rows(lax.all_gather(own_cols, "fsdp", axis=0, tiled=True))
    projected = own_part + received
    keys_values = projected.astype(jnp.bfloat16)
    partial_score = jnp.dot(projected, readout, precision=lax.Precision.HIGHEST)
    token_score = lax.psum(partial_score, ("tp", "sect"))
    mask_float = prompt_mask.astype(jnp.float32)
    row_len = lengths[0]
    finish = jnp.cumsum(row_len)
    starts = finish - row_len
    places = jnp.arange(tok_rows, dtype=jnp.int32)
    member = ((places[None, :] >= starts[:, None]) & (places[None, :] < finish[:, None])).astype(
        jnp.float32
    )
    seq_sum = jnp.dot(member, token_score * mask_float, precision=lax.Precision.HIGHEST)
    count = jnp.dot(member, mask_float, precision=lax.Precision.HIGHEST)
    reward = seq_sum / jnp.sqrt(jnp.maximum(count, 1.0))
    group_count = group_ids.shape[0] * lax.axis_size("fsdp") // 8
    onehot = (group_ids[:, None] == jnp.arange(group_count, dtype=jnp.int32)[None, :]).astype(
        jnp.float32
    )
    local_sizes = jnp.sum(onehot, axis=0)
    local_sums = jnp.sum(onehot * reward[:, None], axis=0)
    group_sums, group_sizes = lax.psum((local_sums, local_sizes), "fsdp")
    mean_g = group_sums / jnp.maximum(group_sizes, 1.0)
    own_mean = jnp.sum(onehot * mean_g[None, :], axis=1)
    local_dev = jnp.sum(onehot * ((reward - own_mean) ** 2)[:, None], axis=0)
    spread = lax.psum(local_dev, "fsdp")
    var_g = spread / jnp.maximum(group_sizes, 1.0)
    own_var = jnp.sum(onehot * var_g[None, :], axis=1)
    advantages = (reward - own_mean) / jnp.sqrt(own_var + 1.0)
    return (keys_values, advantages)


def solution(mesh):
    return jax.shard_map(
        local,
        mesh=mesh,
        in_specs=(
            P("fsdp", "sect"),
            P(("sect", "fsdp"), "tp"),
            P(("tp", "sect")),
            P("fsdp", None),
            P("fsdp"),
            P("fsdp"),
        ),
        out_specs=(P("fsdp", ("tp", "sect")), P("fsdp")),
        check_vma=False,
    )
```

profile of v0, /device:TPU:0, one launch (start us, length us, event | category | flops | bytes accessed | tf_op | source)
XLA Modules:
  0.0 153.3 jit_solution(12628619160099686405)
XLA Ops:
  7.2 0.0 all-gather.5.cloned.1.call-start
  7.2 2.2 %constant_dynamic-slice_fusion.1 = (bf16[1024,256]{1,0:T(8,128)(2,1)}, bf16[1024,256]{1,0:T(8,128)(2,1)}) fusion(bf16[1024,512]{1,0:T(8,128)(2,1)} %param.7, s32[]{:T(128)S(6)} %select_n.6, s32[]{:T(128)S(6)} %select_n.7), kind=kLoop, calls=%fused_computation.20 | loop fusion | bytes 2097160 | tf_op jit(solution)/shard_map/dynamic_slice | solution.py:25
  9.5 0.0 all-gather.5.cloned.1.call-update
  9.5 0.0 all-gather.3.cloned.1.call-start
  9.5 0.7 all-gather.3.cloned.1.call-update
  10.3 47.8 %all-gather.5.cloned.1.call-done = bf16[4096,256]{1,0:T(8,128)(2,1)} async-done(((bf16[1024,256]{1,0:T(8,128)(2,1)}), bf16[4096,256]{1,0:T(8,128)(2,1)}) %all-gather.5.cloned.1.call-update) | async-done | bytes 2097168 | tf_op jit(solution)/shard_map/all_gather | solution.py:23
  58.0 6.4 %convolution_bitcast_fusion = f32[1024,256]{0,1:T(8,128)S(1)} fusion(bf16[4096,256]{1,0:T(8,128)(2,1)} %all-gather.5.cloned.1.call-done, bf16[1024,4096]{1,0:T(8,128)(2,1)} %param.6), kind=kOutput, calls=%fused_computation | convolution fusion | flops 2147483648 | bytes 11534336 | tf_op jit(solution)/shard_map/dot_general | solution.py:20
  64.4 1.5 collective-permute-start
  66.0 0.2 reduce-window.7
  66.2 38.5 %all-gather.3.cloned.1.call-done = bf16[4096,256]{1,0:T(8,128)(2,1)} async-done(((bf16[1024,256]{1,0:T(8,128)(2,1)}), bf16[4096,256]{1,0:T(8,128)(2,1)}) %all-gather.3.cloned.1.call-update) | async-done | bytes 2097168 | tf_op jit(solution)/shard_map/all_gather | solution.py:26
  104.7 6.4 %fusion.8 = (bf16[1024,256]{0,1:T(8,128)(2,1)S(1)}, f32[1024,256]{0,1:T(8,128)S(1)}) fusion(f32[1024,256]{0,1:T(8,128)S(1)} %collective-permute-done, bf16[4096,256]{1,0:T(8,128)(2,1)} %all-gather.3.cloned.1.call-done, bf16[1024,4096]{1,0:T(8,128)(2,1)} %param.6), kind=kOutput, calls=%fused_computation.25 | convolution fusion | flops 2148007936 | bytes 13107200 | tf_op jit(solution)/shard_map/dot_general | solution.py:20
  111.1 0.6 fusion.9
  111.8 13.5 %psum.28 = f32[1024]{0:T(1024)S(1)} all-reduce(f32[1024]{0:T(1024)S(1)} %bitcast.34), channel_id=1, replica_groups=mesh['fsdp'=4,'tp'=4,'sect'=2] {'tp','sect'}, use_global_device_ids=true, to_apply=%region_1.0 | all-reduce | flops 1024 | bytes 8192 | tf_op jit(solution)/shard_map/psum | solution.py:30
  125.3 0.2 convolution_bitcast_fusion.3
  125.5 0.2 fusion.3
  125.7 0.0 copy-done.2
  125.7 0.2 convert_reduce_fusion
  125.9 9.8 %all-reduce = (f32[2]{0:T(128)S(1)}, f32[2]{0:T(128)S(1)}) all-reduce(f32[2]{0:T(128)S(1)} %get-tuple-element.7, f32[2]{0:T(128)S(1)} %get-tuple-element.6), channel_id=1, replica_groups=mesh['fsdp'=4,'tp'=4,'sect'=2] {'fsdp'}, use_global_device_ids=true, to_apply=%region_3.4 | all-reduce | flops 4 | bytes 32 | tf_op jit(solution)/shard_map/psum | solution.py:48
  135.7 0.1 select_reduce_fusion.2
  135.8 0.1 select_reduce_fusion.1
  135.9 8.9 %psum.31 = f32[2]{0:T(128)S(1)} all-reduce(f32[2]{0:T(128)S(1)} %select_reduce_fusion.1), channel_id=1, replica_groups=mesh['fsdp'=4,'tp'=4,'sect'=2] {'fsdp'}, use_global_device_ids=true, to_apply=%region_8.9 | all-reduce | flops 2 | bytes 16 | tf_op jit(solution)/shard_map/psum | solution.py:52
  144.9 0.1 select_reduce_fusion
  145.0 1.0 copy.9
  146.0 0.5 rsqrt_multiply_fusion
  (14 shorter events, 0.1 us)
Async XLA Ops:
  7.2 104.0 %copy-start = (f32[256]{0:T(256)S(1)}, f32[256]{0:T(256)}, u32[]{:S(2)}) copy-start(f32[256]{0:T(256)} %param.8) | copy-start | bytes 3076
  7.2 50.9 %all-gather.5.cloned.1.call-start = ((), (), s32[]{:S(2)}) async-start(), calls=%async_computation.1 | async-start | bytes 2621440 | tf_op jit(solution)/shard_map/all_gather | solution.py:23
  9.5 95.2 %all-gather.3.cloned.1.call-start = ((), (), s32[]{:S(2)}) async-start(), calls=%async_computation | async-start | bytes 2621440 | tf_op jit(solution)/shard_map/all_gather | solution.py:26
  10.2 55.7 %copy-start.3 = (s32[1,4]{1,0:T(1,128)S(1)}, s32[1,4]{1,0:T(1,128)}, u32[]{:S(2)}) copy-start(s32[1,4]{1,0:T(1,128)} %param.9) | copy-start | bytes 52
  10.3 55.9 %copy-start.1 = (s32[1024]{0:T(1024)S(1)}, s32[1024]{0:T(1024)}, u32[]{:S(2)}) copy-start(s32[1024]{0:T(1024)} %param.10) | copy-start | bytes 12292
  64.4 40.3 %collective-permute-start = (f32[1024,256]{0,1:T(8,128)S(1)}, f32[1024,256]{0,1:T(8,128)S(1)}, u32[]{:S(2)}, u32[]{:S(2)}) collective-permute-start(f32[1024,256]{0,1:T(8,128)S(1)} %convolution_bitcast_fusion), channel_id=1, source_target_pairs={{0,1},{1,0},{2,3},{3,2},{4,5},{5,4},{6,7},{7,6},{8,9},{9,8},{10,11... | collective-permute-start | bytes 3145736 | tf_op jit(solution)/shard_map/ppermute | solution.py:10
  66.2 59.6 %copy-start.2 = (s32[4]{0:T(128)S(1)}, s32[4]{0:T(128)}, u32[]{:S(2)}) copy-start(s32[4]{0:T(128)} %param.11) | copy-start | bytes 52
Sparse Core Ops, SparseCore 0:
  9.6 48.3 all-gather.4
  60.2 44.4 all-gather.2
where the time goes:
time: 154 us; the launch traced here: 153 us
  waiting for transfers between devices  87 us (56%)
  blocking collectives  32.3 us (21%)
  between operations  14.1 us (9%)
  matrix products  13.9 us (9%)
  local copies, waits for them, and re-layouts  3.28 us (2%)
  starting transfers between devices  1.61 us (1%)
    all_gather x1, waiting for transfers between devices, local(): lax.all_gather(partner_cols, 'fsdp', axis=0, tiled=True)  47.8 us
    all_gather x1, waiting for transfers between devices, local(): own_part = add_rows(lax.all_gather(own_cols, 'fsdp', axis=0, tiled=True))  38.5 us
    psum x1, blocking collectives, local(): token_score = lax.psum(partial_score, ('tp', 'sect'))  13.5 us
    dot_general x2, matrix products, add_rows(): return jnp.dot(hidden, piece, preferred_element_type=jnp.float32)  12.8 us
    psum x1, blocking collectives, local(): group_sums, group_sizes = lax.psum((local_sums, local_sizes), 'fsdp')  9.81 us
    psum x1, blocking collectives, local(): spread = lax.psum(local_dev, 'fsdp')  8.94 us
  transfers between devices with their start and end apart: 3, of which 2 were waited for; matrix products, arithmetic and copies ran while one was open for 4% of the time, Pallas kernels for 0%

commit v1 on v0

--- a/solution.py
+++ b/solution.py
@@ -27,7 +27,7 @@
     projected = own_part + received
     keys_values = projected.astype(jnp.bfloat16)
     partial_score = jnp.dot(projected, readout, precision=lax.Precision.HIGHEST)
-    token_score = lax.psum(partial_score, ("tp", "sect"))
+    token_score = lax.psum(lax.psum(partial_score, "sect"), "tp")
     mask_float = prompt_mask.astype(jnp.float32)
     row_len = lengths[0]
     finish = jnp.cumsum(row_len)

time: 154 us -> 151 us (0.981)
  blocking collectives: 32.3 us -> 29.3 us
    psum x1 -> x2, blocking collectives: 13.5 us -> 10.6 us  [local(): token_score = lax.psum(lax.psum(partial_score, 'sect'), 'tp')]
where the time goes in v1:
time: 151 us; the launch traced here: 150 us
  waiting for transfers between devices  87 us (58%)
  blocking collectives  29.3 us (19%)
  between operations  14.1 us (9%)
  matrix products  13.9 us (9%)
  local copies, waits for them, and re-layouts  3.28 us (2%)
  starting transfers between devices  1.61 us (1%)
    all_gather x1, waiting for transfers between devices, local(): lax.all_gather(partner_cols, 'fsdp', axis=0, tiled=True)  47.8 us
    all_gather x1, waiting for transfers between devices, local(): own_part = add_rows(lax.all_gather(own_cols, 'fsdp', axis=0, tiled=True))  38.5 us
    dot_general x2, matrix products, add_rows(): return jnp.dot(hidden, piece, preferred_element_type=jnp.float32)  12.8 us
    psum x2, blocking collectives, local(): token_score = lax.psum(lax.psum(partial_score, 'sect'), 'tp')  10.6 us
    psum x1, blocking collectives, local(): group_sums, group_sizes = lax.psum((local_sums, local_sizes), 'fsdp')  9.75 us
    psum x1, blocking collectives, local(): spread = lax.psum(local_dev, 'fsdp')  9 us
  transfers between devices with their start and end apart: 3, of which 2 were waited for; matrix products, arithmetic and copies ran while one was open for 4% of the time, Pallas kernels for 0%

profile of v1, /device:TPU:0, one launch (start us, length us, event | category | flops | bytes accessed | tf_op | source)
XLA Modules:
  0.0 150.4 jit_solution(6823630262091178777)
XLA Ops:
  7.2 0.0 all-gather.5.cloned.1.call-start
  7.2 2.2 %constant_dynamic-slice_fusion.1 = (bf16[1024,256]{1,0:T(8,128)(2,1)}, bf16[1024,256]{1,0:T(8,128)(2,1)}) fusion(bf16[1024,512]{1,0:T(8,128)(2,1)} %param.7, s32[]{:T(128)S(6)} %select_n.6, s32[]{:T(128)S(6)} %select_n.7), kind=kLoop, calls=%fused_computation.20 | loop fusion | bytes 2097160 | tf_op jit(solution)/shard_map/dynamic_slice | solution.py:25
  9.5 0.0 all-gather.5.cloned.1.call-update
  9.5 0.0 all-gather.3.cloned.1.call-start
  9.5 0.7 all-gather.3.cloned.1.call-update
  10.3 47.8 %all-gather.5.cloned.1.call-done = bf16[4096,256]{1,0:T(8,128)(2,1)} async-done(((bf16[1024,256]{1,0:T(8,128)(2,1)}), bf16[4096,256]{1,0:T(8,128)(2,1)}) %all-gather.5.cloned.1.call-update) | async-done | bytes 2097168 | tf_op jit(solution)/shard_map/all_gather | solution.py:23
  58.0 6.4 %convolution_bitcast_fusion = f32[1024,256]{0,1:T(8,128)S(1)} fusion(bf16[4096,256]{1,0:T(8,128)(2,1)} %all-gather.5.cloned.1.call-done, bf16[1024,4096]{1,0:T(8,128)(2,1)} %param.6), kind=kOutput, calls=%fused_computation | convolution fusion | flops 2147483648 | bytes 11534336 | tf_op jit(solution)/shard_map/dot_general | solution.py:20
  64.4 1.5 %collective-permute-start = (f32[1024,256]{0,1:T(8,128)S(1)}, f32[1024,256]{0,1:T(8,128)S(1)}, u32[]{:S(2)}, u32[]{:S(2)}) collective-permute-start(f32[1024,256]{0,1:T(8,128)S(1)} %convolution_bitcast_fusion), channel_id=1, source_target_pairs={{0,1},{1,0},{2,3},{3,2},{4,5},{5,4},{6,7},{7,6},{8,9},{9,8},{10,11... | collective-permute-start | bytes 3145736 | tf_op jit(solution)/shard_map/ppermute | solution.py:10
  66.0 0.2 reduce-window.7
  66.2 38.5 %all-gather.3.cloned.1.call-done = bf16[4096,256]{1,0:T(8,128)(2,1)} async-done(((bf16[1024,256]{1,0:T(8,128)(2,1)}), bf16[4096,256]{1,0:T(8,128)(2,1)}) %all-gather.3.cloned.1.call-update) | async-done | bytes 2097168 | tf_op jit(solution)/shard_map/all_gather | solution.py:26
  104.7 6.4 %fusion.8 = (bf16[1024,256]{0,1:T(8,128)(2,1)S(1)}, f32[1024,256]{0,1:T(8,128)S(1)}) fusion(f32[1024,256]{0,1:T(8,128)S(1)} %collective-permute-done, bf16[4096,256]{1,0:T(8,128)(2,1)} %all-gather.3.cloned.1.call-done, bf16[1024,4096]{1,0:T(8,128)(2,1)} %param.6), kind=kOutput, calls=%fused_computation.25 | convolution fusion | flops 2148007936 | bytes 13107200 | tf_op jit(solution)/shard_map/dot_general | solution.py:20
  111.1 0.6 fusion.9
  111.8 4.9 %psum.35 = f32[1024]{0:T(1024)S(1)} all-reduce(f32[1024]{0:T(1024)S(1)} %bitcast.34), channel_id=1, replica_groups=mesh['fsdp'=4,'tp'=4,'sect'=2] {'sect'}, use_global_device_ids=true, to_apply=%region_1.0 | all-reduce | flops 1024 | bytes 8192 | tf_op jit(solution)/shard_map/psum | solution.py:30
  116.7 5.6 %psum.36 = f32[1024]{0:T(1024)S(1)} all-reduce(f32[1024]{0:T(1024)S(1)} %psum.35), channel_id=1, replica_groups=mesh['fsdp'=4,'tp'=4,'sect'=2] {'tp'}, use_global_device_ids=true, to_apply=%region_2.0 | all-reduce | flops 1024 | bytes 8192 | tf_op jit(solution)/shard_map/psum | solution.py:30
  122.3 0.2 convolution_bitcast_fusion.3
  122.5 0.2 fusion.3
  122.8 0.2 convert_reduce_fusion
  122.9 9.8 %all-reduce = (f32[2]{0:T(128)S(1)}, f32[2]{0:T(128)S(1)}) all-reduce(f32[2]{0:T(128)S(1)} %get-tuple-element.7, f32[2]{0:T(128)S(1)} %get-tuple-element.6), channel_id=1, replica_groups=mesh['fsdp'=4,'tp'=4,'sect'=2] {'fsdp'}, use_global_device_ids=true, to_apply=%region_4.5 | all-reduce | flops 4 | bytes 32 | tf_op jit(solution)/shard_map/psum | solution.py:48
  132.7 0.1 select_reduce_fusion.2
  132.8 0.1 select_reduce_fusion.1
  132.9 9.0 %psum.39 = f32[2]{0:T(128)S(1)} all-reduce(f32[2]{0:T(128)S(1)} %select_reduce_fusion.1), channel_id=1, replica_groups=mesh['fsdp'=4,'tp'=4,'sect'=2] {'fsdp'}, use_global_device_ids=true, to_apply=%region_9.10 | all-reduce | flops 2 | bytes 16 | tf_op jit(solution)/shard_map/psum | solution.py:52
  141.9 0.1 select_reduce_fusion
  142.0 1.0 copy.9
  143.0 0.5 rsqrt_multiply_fusion
  (15 shorter events, 0.1 us)
Async XLA Ops:
  7.2 104.0 %copy-start = (f32[256]{0:T(256)S(1)}, f32[256]{0:T(256)}, u32[]{:S(2)}) copy-start(f32[256]{0:T(256)} %param.8) | copy-start | bytes 3076
  7.2 50.9 %all-gather.5.cloned.1.call-start = ((), (), s32[]{:S(2)}) async-start(), calls=%async_computation.1 | async-start | bytes 2621440 | tf_op jit(solution)/shard_map/all_gather | solution.py:23
  9.5 95.2 %all-gather.3.cloned.1.call-start = ((), (), s32[]{:S(2)}) async-start(), calls=%async_computation | async-start | bytes 2621440 | tf_op jit(solution)/shard_map/all_gather | solution.py:26
  10.2 55.7 %copy-start.3 = (s32[1,4]{1,0:T(1,128)S(1)}, s32[1,4]{1,0:T(1,128)}, u32[]{:S(2)}) copy-start(s32[1,4]{1,0:T(1,128)} %param.9) | copy-start | bytes 52
  10.3 55.9 %copy-start.1 = (s32[1024]{0:T(1024)S(1)}, s32[1024]{0:T(1024)}, u32[]{:S(2)}) copy-start(s32[1024]{0:T(1024)} %param.10) | copy-start | bytes 12292
  64.4 40.3 %collective-permute-start = (f32[1024,256]{0,1:T(8,128)S(1)}, f32[1024,256]{0,1:T(8,128)S(1)}, u32[]{:S(2)}, u32[]{:S(2)}) collective-permute-start(f32[1024,256]{0,1:T(8,128)S(1)} %convolution_bitcast_fusion), channel_id=1, source_target_pairs={{0,1},{1,0},{2,3},{3,2},{4,5},{5,4},{6,7},{7,6},{8,9},{9,8},{10,11... | collective-permute-start | bytes 3145736 | tf_op jit(solution)/shard_map/ppermute | solution.py:10
  66.2 56.6 %copy-start.2 = (s32[4]{0:T(128)S(1)}, s32[4]{0:T(128)}, u32[]{:S(2)}) copy-start(s32[4]{0:T(128)} %param.11) | copy-start | bytes 52
Sparse Core Ops, SparseCore 0:
  9.6 48.3 all-gather.4
  60.2 44.4 all-gather.2
